TPU v7x, 256 devices: a whole 4x4x8 slice. The times are simulated.
256 devices in a mesh: seq: 32 (over y, x, core), tp: 8 (over z).
Axes of the slice: x: 4, y: 4, z: 8, core: 2. Of those that a mesh axis runs over, the one named last changes fastest.
Arguments:
- tokens: bfloat16 [8192, 4096], P('seq', 'tp'), may hold values from -11 to 11
- grad_out: bfloat16 [8192, 4096], P('seq', 'tp'), may hold values from -1.5 to 1.5
- in_weight: bfloat16 [4096, 4096], P('seq', 'tp'), may hold values from -0.09880682 to 0.09880682
- in_scale: float32 [4096], P('tp'), may hold values from 0.0008238636 to 0.010511364
- out_weight: bfloat16 [4096, 4096], P('seq', 'tp'), may hold values from -0.053943182 to 0.053943182
- out_scale: float32 [4096], replicated, may hold values from 0.00139204545 to 0.0057386364
- state_in: bfloat16 [8192, 128], P('seq'), may hold values from -0.0625 to 0.0625
- state_out: bfloat16 [8192, 128], P('seq'), may hold values from -6 to 6
- log_decay: float32 [8192, 64], P('seq', 'tp'), may hold values from -1.6 to 0
Outputs:
- grad_tokens: bfloat16 [8192, 4096], P('seq', 'tp')
- grad_in_weight: float32 [4096, 4096], P('seq', 'tp')
- grad_in_scale: float32 [4096], P('tp')
- grad_out_weight: float32 [4096, 4096], P('seq', 'tp')
- grad_out_scale: float32 [4096], P('seq')
All inputs are finite; a program needn't handle non-finite values.
Results may differ from a plain program's by a relative error of at most 0.027.
Values may be sent and summed in bfloat16 or wider, within the bound.
No kernel may reach another device: no remote copies, remote signals or barrier semaphores. Data moves between devices by JAX's collectives and lax.ppermute only.
A program may use at most 128 MiB of HBM per device.

v0:
```python
import jax
import jax.numpy as jnp
from jax import lax
from jax.sharding import PartitionSpec as P

D = 4096
HEADS = 64
HEAD_DIM = 64
STRETCH = 256
QMAX = 7
precise = lax.Precision.HIGHEST


def prefix(array, axis, join, neutral, backward):
    count = lax.axis_size(axis)
    place = lax.axis_index(axis)
    ahead = count - 1 - place if backward else place
    gathered = jax.tree.map(
        lambda a, kind: lax.all_gather(a.astype(kind), axis), array, (jnp.bfloat16, jnp.bfloat16)
    )
    state = jax.tree.map(lambda a, e: jnp.zeros_like(a) + jnp.asarray(e, a.dtype), array, neutral)

    def one(turn, state):
        source = count - 1 - turn if backward else turn
        return join(
            state,
            jax.tree.map(
                lambda a, own: lax.dynamic_index_in_dim(a, source, 0, False).astype(own.dtype),
                gathered,
                array,
            ),
        )

    return lax.fori_loop(0, ahead, one, state)


def quantize(weight, channel_scale):
    ratios = weight.astype(jnp.float32) / channel_scale
    clipped = jnp.clip(ratios, -QMAX, QMAX)
    levels = jnp.floor(clipped + 0.5)
    inside = jnp.abs(ratios) <= QMAX
    slopes = jnp.where(inside, levels - ratios, levels)
    return (levels, slopes, inside.astype(jnp.float32))


def stretch_terms(decay_logs, inputs_f, outputs_f):
    cumul = jnp.cumsum(decay_logs, axis=0)
    ending = cumul[-1]
    spread = cumul[:, None, :] - cumul[None, :, :]
    length = decay_logs.shape[0]
    causal = jnp.arange(length)[:, None] >= jnp.arange(length)[None, :]
    mixing = jnp.exp(jnp.where(causal[:, :, None], spread, -jnp.inf))
    intersection = jnp.dot(outputs_f, inputs_f.T, precision=precise)
    return (cumul, ending, mixing * intersection[:, :, None])


def forward_step(carried, pieces):
    values, cumul, ending, weights, inputs_f, outputs_f = pieces
    inner = jnp.einsum("sth,thp->shp", weights, values, precision=precise)
    outer = jnp.exp(cumul)[:, :, None] * jnp.einsum(
        "sn,hnp->shp", outputs_f, carried, precision=precise
    )
    fresh = jnp.einsum(
        "th,tn,thp->hnp", jnp.exp(ending[None, :] - cumul), inputs_f, values, precision=precise
    )
    return (jnp.exp(ending)[:, None, None] * carried + fresh, inner + outer)


def backward_step(carried, pieces):
    grads, cumul, ending, weights, inputs_f, outputs_f = pieces
    inner = jnp.einsum("sth,shp->thp", weights, grads, precision=precise)
    outer = jnp.exp(ending[None, :] - cumul)[:, :, None] * jnp.einsum(
        "tn,hnp->thp", inputs_f, carried, precision=precise
    )
    fresh = jnp.einsum("sh,sn,shp->hnp", jnp.exp(cumul), outputs_f, grads, precision=precise)
    return (jnp.exp(ending)[:, None, None] * carried + fresh, inner + outer)


def join_forward(earlier, later):
    return (earlier[0] * later[0], later[0][:, None, None] * earlier[1] + later[1])


def join_backward(earlier, later):
    return (earlier[0] * later[0], later[1] + later[0][:, None, None] * earlier[1])


def per_device(
    tokens, grad_out, in_weight, in_scale, out_weight, out_scale, state_in, state_out, log_decay
):
    local_rows = tokens.shape[0]
    heads_here = log_decay.shape[1]
    width_here = in_scale.shape[0]
    head_size = width_here // heads_here
    state_size = state_in.shape[1]
    weight_rows = in_weight.shape[0]
    blocks = local_rows // STRETCH
    row_start = lax.axis_index("seq") * weight_rows
    out_scale_rows = lax.dynamic_slice_in_dim(out_scale, row_start, weight_rows)
    in_levels, in_slopes, in_inside = quantize(in_weight, in_scale[None, :])
    out_levels, out_slopes, out_inside = quantize(out_weight, out_scale_rows[:, None])
    in_codes = lax.all_gather(in_levels.astype(jnp.bfloat16), "seq", axis=0, tiled=True)
    out_codes = lax.all_gather(out_levels.astype(jnp.bfloat16), "seq", axis=0, tiled=True)
    features = lax.all_gather(tokens, "tp", axis=1, tiled=True)
    cotangent = lax.all_gather(grad_out, "tp", axis=1, tiled=True)
    projected = jnp.dot(features, in_codes, preferred_element_type=jnp.float32) * in_scale[None, :]
    scaled_grad = (cotangent.astype(jnp.float32) * out_scale[None, :]).astype(jnp.bfloat16)
    grad_mixed = jnp.dot(scaled_grad, out_codes, preferred_element_type=jnp.float32)
    inputs_full = state_in.astype(jnp.float32)
    outputs_full = state_out.astype(jnp.float32)
    decay_blocks = log_decay.reshape(blocks, STRETCH, heads_here)
    input_blocks = inputs_full.reshape(blocks, STRETCH, state_size)
    output_blocks = outputs_full.reshape(blocks, STRETCH, state_size)
    cumul, ending, weights = jax.vmap(stretch_terms)(decay_blocks, input_blocks, output_blocks)
    value_blocks = projected.reshape(blocks, STRETCH, heads_here, head_size)
    grad_blocks = grad_mixed.reshape(blocks, STRETCH, heads_here, head_size)
    empty = jnp.zeros((heads_here, state_size, head_size), jnp.float32)
    local_state, mixed_local = lax.scan(
        forward_step, empty, (value_blocks, cumul, ending, weights, input_blocks, output_blocks)
    )
    local_grad_state, grad_local = lax.scan(
        backward_step,
        empty,
        (grad_blocks, cumul, ending, weights, input_blocks, output_blocks),
        reverse=True,
    )
    running = jnp.cumsum(log_decay, axis=0)
    device_total = running[-1]
    device_decay = jnp.exp(device_total)
    identity = (jnp.ones_like(device_decay), empty)
    entering = prefix((device_decay, local_state), "seq", join_forward, identity, False)[1]
    leaving = prefix((device_decay, local_grad_state), "seq", join_backward, identity, True)[1]
    mixed = mixed_local.reshape(local_rows, heads_here, head_size) + jnp.exp(running)[
        :, :, None
    ] * jnp.einsum("tn,hnp->thp", outputs_full, entering, precision=precise)
    grad_values = grad_local.reshape(local_rows, heads_here, head_size) + jnp.exp(
        device_total[None, :] - running
    )[:, :, None] * jnp.einsum("tn,hnp->thp", inputs_full, leaving, precision=precise)
    mixed = mixed.reshape(local_rows, width_here)
    grad_values = grad_values.reshape(local_rows, width_here)
    mixed_b = mixed.astype(jnp.bfloat16)
    grad_b = grad_values.astype(jnp.bfloat16)
    grad_scaled = (grad_values * in_scale[None, :]).astype(jnp.bfloat16)
    piece = features
    in_total = lax.psum_scatter(
        jnp.einsum("td,tc->dc", piece, grad_b, preferred_element_type=jnp.float32).astype(
            jnp.bfloat16
        ),
        "seq",
        scatter_dimension=0,
        tiled=True,
    ).astype(jnp.float32)
    piece = cotangent
    out_total = lax.psum_scatter(
        jnp.einsum("td,tc->dc", piece, mixed_b, preferred_element_type=jnp.float32).astype(
            jnp.bfloat16
        ),
        "seq",
        scatter_dimension=0,
        tiled=True,
    ).astype(jnp.float32)
    partial_tokens = jnp.einsum(
        "tc,dc->td", grad_scaled, in_codes, preferred_element_type=jnp.float32
    )
    grad_tokens = lax.psum_scatter(
        partial_tokens.astype(jnp.bfloat16), "tp", scatter_dimension=1, tiled=True
    )
    in_part = jnp.sum(in_total * in_slopes, axis=0)
    out_part = jnp.sum(out_total * out_slopes, axis=1)
    in_sum = lax.psum(in_part, "seq")
    out_sum = lax.psum(out_part, "tp")
    grad_in_scale = in_sum / jnp.sqrt(jnp.float32(D * QMAX))
    grad_out_scale = out_sum / jnp.sqrt(jnp.float32(HEADS * HEAD_DIM * QMAX))
    return (
        grad_tokens,
        in_total * in_inside,
        grad_in_scale,
        out_total * out_inside,
        grad_out_scale,
    )


def solution(mesh):
    placed = (
        P("seq", "tp"),
        P("seq", "tp"),
        P("seq", "tp"),
        P("tp"),
        P("seq", "tp"),
        P(),
        P("seq", None),
        P("seq", None),
        P("seq", "tp"),
    )
    return jax.shard_map(
        per_device,
        mesh=mesh,
        in_specs=placed,
        out_specs=(P("seq", "tp"), P("seq", "tp"), P("tp"), P("seq", "tp"), P("seq")),
        check_vma=False,
    )
```

profile of v0, /device:TPU:6, one launch (start us, length us, event | category | flops | bytes accessed | tf_op | source)
XLA Modules:
  0.0 612.6 jit_solution(15400213899961906926)
XLA Ops:
  8.0 1.0 copy.60
  10.5 1.3 reduce-window.14
  12.4 41.5 %all-gather.10.cloned.1.call-done = bf16[256,4096]{1,0:T(8,128)(2,1)} async-done(((bf16[256,512]{1,0:T(8,128)(2,1)}), bf16[256,4096]{1,0:T(8,128)(2,1)}) %all-gather.10.cloned.1.call-update) | async-done | bytes 2097168 | tf_op jit(solution)/shard_map/all_gather | solution.py:104
  53.9 55.4 %all-gather.12.cloned.1.call-done = bf16[4096,512]{0,1:T(8,128)(2,1)} async-done(((bf16[128,512]{0,1:T(8,128)(2,1)}), bf16[4096,512]{0,1:T(8,128)(2,1)}) %all-gather.12.cloned.1.call-update) | async-done | bytes 4194320 | tf_op jit(solution)/shard_map/all_gather | solution.py:102
  109.3 4.1 fusion.2
  113.4 1.0 fusion.20
  116.2 18.9 %all-gather.2 = bf16[32,1,8]{2,1,0:T(2,128)(2,1)S(1)} all-gather(bf16[1,1,8]{2,1,0:T(2,128)(2,1)S(1)} %bitcast.154), channel_id=1, replica_groups=mesh['seq'=32,'tp'=8] {'seq'}, dimensions={0}, use_global_device_ids=true | all-gather | bytes 528 | tf_op jit(solution)/shard_map/all_gather | solution.py:19
  135.6 1.8 fusion.6
  137.5 28.1 %all-gather.18.cloned.1.call-done = bf16[256,128,64]{1,2,0:T(8,128)(2,1)} async-done(((bf16[8,128,64]{1,2,0:T(8,128)(2,1)}), bf16[256,128,64]{1,2,0:T(8,128)(2,1)}) %all-gather.18.cloned.1.call-update) | async-done | bytes 4194320 | tf_op jit(solution)/shard_map/all_gather | solution.py:19
  165.6 32.6 %while.16 = (s32[]{:T(128)}, f32[8,128,64]{2,1,0:T(8,128)S(1)}, s32[]{:T(128)}, bf16[32,8,128,64]{2,3,1,0:T(8,128)(2,1)}, bf16[32,8]{1,0:T(8,128)(2,1)S(1)}, /*index=5*/s32[]{:T(128)}, s32[]{:T(128)}, s32[]{:T(128)}, s32[]{:T(128)}) while((s32[]{:T(128)}, f32[8,128,64]{2,1,0:T(8,128)S(1)}, s32[]{:T(128)}, bf16[32,8,128,64]{2,3,1,0:T(8,128)(2,1)}, ...), condition=%wide.region_5.6_spmd, body=%wide.region_4.5_spmd.sunk | while | flops 196622 | bytes 1179883 | solution.py:34
  165.6 0.9 constant_dynamic-slice_fusion.4
  166.9 0.9 constant_dynamic-slice_fusion.4
  168.2 0.9 constant_dynamic-slice_fusion.4
  170.8 0.9 constant_dynamic-slice_fusion.4
  172.1 0.9 constant_dynamic-slice_fusion.4
  173.4 0.9 constant_dynamic-slice_fusion.4
  174.7 0.9 constant_dynamic-slice_fusion.4
  177.3 0.9 constant_dynamic-slice_fusion.4
  179.9 0.9 constant_dynamic-slice_fusion.4
  181.3 0.9 constant_dynamic-slice_fusion.4
  182.6 0.9 constant_dynamic-slice_fusion.4
  183.9 0.9 constant_dynamic-slice_fusion.4
  185.2 0.9 constant_dynamic-slice_fusion.4
  187.8 0.9 constant_dynamic-slice_fusion.4
  189.1 0.9 constant_dynamic-slice_fusion.4
  191.7 0.9 constant_dynamic-slice_fusion.4
  193.0 0.9 constant_dynamic-slice_fusion.4
  195.6 0.9 constant_dynamic-slice_fusion.4
  196.9 0.9 constant_dynamic-slice_fusion.4
  199.3 8.6 %all-gather.16.cloned.1.call-done = bf16[256,4096]{1,0:T(8,128)(2,1)} async-done(((bf16[256,512]{1,0:T(8,128)(2,1)}), bf16[256,4096]{1,0:T(8,128)(2,1)}) %all-gather.16.cloned.1.call-update) | async-done | bytes 2097168 | tf_op jit(solution)/shard_map/all_gather | solution.py:103
  207.9 4.8 fusion
  212.7 6.5 %copy.81 = bf16[4096,512]{1,0:T(8,128)(2,1)} copy(bf16[4096,512]{0,1:T(8,128)(2,1)} %fusion) | data formatting | bytes 8388608
  220.2 87.2 %reduce-scatter.10.cloned.1.call-done = bf16[128,512]{1,0:T(8,128)(2,1)} async-done(((bf16[4096,512]{1,0:T(8,128)(2,1)}), bf16[128,512]{1,0:T(8,128)(2,1)}) %reduce-scatter.10.cloned.1.call-update) | async-done | bytes 131088
  307.4 1.0 copy.82
  309.3 54.8 %all-gather.14.cloned.1.call-done = bf16[4096,512]{0,1:T(8,128)(2,1)} async-done(((bf16[128,512]{0,1:T(8,128)(2,1)}), bf16[4096,512]{0,1:T(8,128)(2,1)}) %all-gather.14.cloned.1.call-update) | async-done | bytes 4194320 | tf_op jit(solution)/shard_map/all_gather | solution.py:101
  364.1 3.5 convolution_multiply_fusion
  368.4 1.0 fusion.19
  369.6 3.5 fusion.7
  373.0 47.4 %all-gather.20.cloned.1.call-done = bf16[256,128,64]{1,2,0:T(8,128)(2,1)} async-done(((bf16[8,128,64]{1,2,0:T(8,128)(2,1)}), bf16[256,128,64]{1,2,0:T(8,128)(2,1)}) %all-gather.20.cloned.1.call-update) | async-done | bytes 4194320 | tf_op jit(solution)/shard_map/all_gather | solution.py:19
  420.5 8.0 %while.17 = (s32[]{:T(128)}, f32[8,128,64]{2,1,0:T(8,128)S(1)}, s32[]{:T(128)}, bf16[32,8]{1,0:T(8,128)(2,1)S(1)}, bf16[32,8,128,64]{2,3,1,0:T(8,128)(2,1)}, /*index=5*/s32[]{:T(128)}, s32[]{:T(128)}, s32[]{:T(128)}) while((s32[]{:T(128)}, f32[8,128,64]{2,1,0:T(8,128)S(1)}, s32[]{:T(128)}, bf16[32,8]{1,0:T(8,128)(2,1)S(1)}, ...), condition=%wide.region_11.12_spmd, body=%wide.region_10.11_spmd.sunk | while | flops 196621 | bytes 1179863 | solution.py:34
  430.1 3.2 fusion.1
  433.4 6.5 %copy.83 = bf16[4096,512]{1,0:T(8,128)(2,1)} copy(bf16[4096,512]{0,1:T(8,128)(2,1)} %fusion.1) | data formatting | bytes 8388608
  440.1 4.9 convolution_convert_fusion.2
  445.8 83.4 %psum.14 = f32[512]{0:T(512)S(1)} all-reduce(f32[512]{0:T(512)S(1)} %get-tuple-element.273), channel_id=1, replica_groups=mesh['seq'=32,'tp'=8] {'seq'}, use_global_device_ids=true, to_apply=%region_9.10 | all-reduce | flops 512 | bytes 4096 | tf_op jit(solution)/shard_map/psum | solution.py:169
  529.8 31.0 %reduce-scatter.12.cloned.1.call-done = bf16[128,512]{1,0:T(8,128)(2,1)} async-done(((bf16[4096,512]{1,0:T(8,128)(2,1)}), bf16[128,512]{1,0:T(8,128)(2,1)}) %reduce-scatter.12.cloned.1.call-update) | async-done | bytes 131088
  560.8 1.0 copy.84
  562.8 17.4 %psum.15 = f32[128]{0:T(128)S(1)} all-reduce(f32[128]{0:T(128)S(1)} %get-tuple-element.275), channel_id=1, replica_groups=mesh['seq'=32,'tp'=8] {'tp'}, use_global_device_ids=true, to_apply=%region_14.15 | all-reduce | flops 128 | bytes 1024 | tf_op jit(solution)/shard_map/psum | solution.py:170
  580.7 25.3 %reduce-scatter.8.cloned.1.call-done = bf16[256,512]{1,0:T(8,128)(2,1)} async-done(((bf16[256,4096]{1,0:T(8,128)(2,1)}), bf16[256,512]{1,0:T(8,128)(2,1)}) %reduce-scatter.8.cloned.1.call-update) | async-done | bytes 262160 | tf_op jit(solution)/shard_map/reduce_scatter | solution.py:164
  (179 shorter events, 35.4 us)
Async XLA Ops:
  7.2 128.3 %copy-start = (bf16[256,128]{1,0:T(8,128)(2,1)S(1)}, bf16[256,128]{1,0:T(8,128)(2,1)}, u32[]{:S(2)}) copy-start(bf16[256,128]{1,0:T(8,128)(2,1)} %param.19) | copy-start | bytes 196612
  7.2 46.7 %all-gather.10.cloned.1.call-start = ((), (), s32[]{:S(2)}) async-start(), calls=%async_computation.3 | async-start | bytes 2359296 | tf_op jit(solution)/shard_map/all_gather | solution.py:104
  7.9 101.4 %all-gather.12.cloned.1.call-start = ((), (), s32[]{:S(2)}) async-start(), calls=%async_computation.4 | async-start | bytes 4325376 | tf_op jit(solution)/shard_map/all_gather | solution.py:102
  10.5 155.0 %all-gather.18.cloned.1.call-start = ((), (), s32[]{:S(2)}) async-start(), calls=%async_computation.8 | async-start | bytes 4325376 | tf_op jit(solution)/shard_map/all_gather | solution.py:19
  12.4 101.1 %copy-start.3 = (bf16[256,128]{1,0:T(8,128)(2,1)S(1)}, bf16[256,128]{1,0:T(8,128)(2,1)}, u32[]{:S(2)}) copy-start(bf16[256,128]{1,0:T(8,128)(2,1)} %param.20) | copy-start | bytes 196612
  12.4 102.8 %copy-start.8 = (f32[256,8]{0,1:T(8,128)S(1)}, f32[256,8]{0,1:T(8,128)}, u32[]{:S(2)}) copy-start(f32[256,8]{0,1:T(8,128)} %param.21) | copy-start | bytes 24580
  114.5 93.4 %all-gather.16.cloned.1.call-start = ((), (), s32[]{:S(2)}) async-start(), calls=%async_computation.7 | async-start | bytes 2359296 | tf_op jit(solution)/shard_map/all_gather | solution.py:103
  115.1 192.3 %reduce-scatter.10.cloned.1.call-start = ((), (), s32[]{:S(2)}) async-start(), calls=%async_computation.10 | async-start | bytes 4325376
  135.6 30.0 %copy-start.5 = (f32[256,256]{1,0:T(8,128)}, f32[256,256]{1,0:T(8,128)S(1)}, u32[]{:S(2)}) copy-start(f32[256,256]{1,0:T(8,128)S(1)} %fusion.57) | copy-start | bytes 786436
  219.2 0.9 copy-start.7
  219.2 89.2 %copy-start.9 = (f32[512]{0:T(512)S(1)}, f32[512]{0:T(512)}, u32[]{:S(2)}) copy-start(f32[512]{0:T(512)} %param.16) | copy-start | bytes 6148
  219.2 145.0 %copy-start.2 = (bf16[256,4096]{1,0:T(8,128)(2,1)S(1)}, bf16[256,4096]{1,0:T(8,128)(2,1)}, u32[]{:S(2)}) copy-start(bf16[256,4096]{1,0:T(8,128)(2,1)} %all-gather.16.cloned.1.call-done) | copy-start | bytes 6291460
  219.2 145.0 %all-gather.14.cloned.1.call-start = ((), (), s32[]{:S(2)}) async-start(), calls=%async_computation.5 | async-start | bytes 4325376 | tf_op jit(solution)/shard_map/all_gather | solution.py:101
  309.3 60.3 %copy-start.6 = (f32[256,256]{1,0:T(8,128)S(1)}, f32[256,256]{1,0:T(8,128)}, u32[]{:S(2)}) copy-start(f32[256,256]{1,0:T(8,128)} %copy-done.5) | copy-start | bytes 786436
  309.3 111.2 %all-gather.20.cloned.1.call-start = ((), (), s32[]{:S(2)}) async-start(), calls=%async_computation.9 | async-start | bytes 4325376 | tf_op jit(solution)/shard_map/all_gather | solution.py:19
  367.6 0.8 copy-start.4
  369.5 191.3 %reduce-scatter.12.cloned.1.call-start = ((), (), s32[]{:S(2)}) async-start(), calls=%async_computation.11 | async-start | bytes 4325376
  428.5 1.6 copy-start.1
  439.9 166.1 %reduce-scatter.8.cloned.1.call-start = ((), (), s32[]{:S(2)}) async-start(), calls=%async_computation.6 | async-start | bytes 2359296 | tf_op jit(solution)/shard_map/reduce_scatter | solution.py:164
Sparse Core Ops, SparseCore 0:
  9.8 44.0 all-gather.9
  56.9 52.3 all-gather.11
  114.6 50.8 all-gather.17
  167.2 40.6 all-gather.15
  219.3 88.0 reduce-scatter.9
  310.6 53.5 all-gather.13
  369.6 50.7 all-gather.19
  440.0 120.7 reduce-scatter.11
  563.9 42.0 reduce-scatter.7
where the time goes:
time: 614 us; the launch traced here: 613 us
  waiting for transfers between devices  381 us (62%)
  blocking collectives  120 us (20%)
  local copies, waits for them, and re-layouts  55.6 us (9%)
  matrix products  30.2 us (5%)
  between operations  14.1 us (2%)
  other arithmetic  10.6 us (2%)
    unnamed x11, waiting for transfers between devices  119 us
    psum x1, blocking collectives, per_device(): in_sum = lax.psum(in_part, 'seq')  83.4 us
    all_gather x2, waiting for transfers between devices, prefix(): lax.all_gather(a.astype(kind), axis)  75.5 us
    all_gather x1, waiting for transfers between devices, per_device(): lax.all_gather(out_levels.astype(jnp.bfloat16), 'seq', axis=0, tiled=True)  55.4 us
    all_gather x1, waiting for transfers between devices, per_device(): lax.all_gather(in_levels.astype(jnp.bfloat16), 'seq', axis=0, tiled=True)  54.8 us
    all_gather x1, waiting for transfers between devices, per_device(): cotangent = lax.all_gather(grad_out, 'tp', axis=1, tiled=True)  41.5 us
    dynamic_slice x62, local copies, waits for them, and re-layouts, one(): lax.dynamic_index_in_dim(a, source, 0, False).astype(own.dtype)  34 us
    reduce_scatter x1, waiting for transfers between devices, per_device(): lax.psum_scatter(partial_tokens.astype(jnp.bfloat16), 'tp', scatter_dimen...  25.3 us
  transfers between devices with their start and end apart: 9, of which 9 were waited for; matrix products, arithmetic and copies ran while one was open for 9% of the time, Pallas kernels for 0%

commit v1 on v0

--- a/solution.py
+++ b/solution.py
@@ -101,7 +101,15 @@
     in_codes = lax.all_gather(in_levels.astype(jnp.bfloat16), "seq", axis=0, tiled=True)
     out_codes = lax.all_gather(out_levels.astype(jnp.bfloat16), "seq", axis=0, tiled=True)
     features = lax.all_gather(tokens, "tp", axis=1, tiled=True)
-    cotangent = lax.all_gather(grad_out, "tp", axis=1, tiled=True)
+    num = jax.lax.axis_size("tp")
+    near = [(jj - 1, jj) for jj in range(1, num)] + [(num - 1, 0)]
+    o_now = grad_out
+    parts_seen = [o_now]
+    for _ in range(num - 1):
+        o_now = jax.lax.ppermute(o_now, "tp", near)
+        parts_seen += [o_now]
+    frame_out = jnp.concatenate([*reversed(parts_seen)], 1)
+    cotangent = jnp.roll(frame_out, (jax.lax.axis_index("tp") + 1) * o_now.shape[1], 1)
     projected = jnp.dot(features, in_codes, preferred_element_type=jnp.float32) * in_scale[None, :]
     scaled_grad = (cotangent.astype(jnp.float32) * out_scale[None, :]).astype(jnp.bfloat16)
     grad_mixed = jnp.dot(scaled_grad, out_codes, preferred_element_type=jnp.float32)

time: 614 us -> 585 us (0.953)
  waiting for transfers between devices: 381 us -> 339 us
    ppermute x0 -> x7, waiting for transfers between devices: none -> 58.5 us  [per_device(): o_now = jax.lax.ppermute(o_now, 'tp', near)]
    all_gather x1, waiting for transfers between devices: 55.4 us -> 0.01 us  [per_device(): lax.all_gather(out_levels.astype(jnp.bfloat16), 'seq', axis=0, tiled=True)]
    all_gather x1 -> x0, waiting for transfers between devices: 41.5 us -> none  [per_device(): cotangent = lax.all_gather(grad_out, 'tp', axis=1, tiled=True)]
    unnamed x28 -> x44, local copies, waits for them, and re-layouts: 20.1 us -> 25.1 us
    unnamed x11 -> x10, waiting for transfers between devices: 119 us -> 119 us
  transfers between devices with their start and end apart: 9 -> 15, of which waited for: 9 -> 14; matrix products, arithmetic and copies ran while one was open for 9% -> 11% of each run, Pallas kernels for 0% -> 0%
where the time goes in v1:
time: 585 us; the launch traced here: 583 us
  waiting for transfers between devices  339 us (58%)
  blocking collectives  122 us (21%)
  local copies, waits for them, and re-layouts  61.3 us (10%)
  matrix products  31.9 us (5%)
  between operations  14.4 us (2%)
  other arithmetic  10.6 us (2%)
    unnamed x10, waiting for transfers between devices  119 us
    psum x1, blocking collectives, per_device(): in_sum = lax.psum(in_part, 'seq')  83.4 us
    all_gather x2, waiting for transfers between devices, prefix(): lax.all_gather(a.astype(kind), axis)  73.5 us
    ppermute x7, waiting for transfers between devices, per_device(): o_now = jax.lax.ppermute(o_now, 'tp', near)  58.5 us
    all_gather x1, waiting for transfers between devices, per_device(): lax.all_gather(in_levels.astype(jnp.bfloat16), 'seq', axis=0, tiled=True)  54.8 us
    dynamic_slice x62, local copies, waits for them, and re-layouts, one(): lax.dynamic_index_in_dim(a, source, 0, False).astype(own.dtype)  34 us
    reduce_scatter x1, waiting for transfers between devices, per_device(): lax.psum_scatter(partial_tokens.astype(jnp.bfloat16), 'tp', scatter_dimen...  25.1 us
    unnamed x44, local copies, waits for them, and re-layouts  25.1 us
  transfers between devices with their start and end apart: 15, of which 14 were waited for; matrix products, arithmetic and copies ran while one was open for 11% of the time, Pallas kernels for 0%

profile of v1, /device:TPU:6, one launch (start us, length us, event | category | flops | bytes accessed | tf_op | source)
XLA Modules:
  0.0 583.2 jit_solution(7646458932287434820)
XLA Ops:
  7.2 1.1 copy.63
  9.9 2.0 collective-permute-start
  11.9 10.5 %collective-permute-done = bf16[256,512]{1,0:T(8,128)(2,1)S(1)} collective-permute-done((bf16[256,512]{1,0:T(8,128)(2,1)}, bf16[256,512]{1,0:T(8,128)(2,1)S(1)}, u32[]{:S(2)}, u32[]{:S(2)}) %collective-permute-start) | collective-permute-done | bytes 262176 | tf_op jit(solution)/shard_map/ppermute | solution.py:109
  22.3 8.7 %collective-permute-done.1 = bf16[256,512]{1,0:T(8,128)(2,1)S(1)} collective-permute-done((bf16[256,512]{1,0:T(8,128)(2,1)S(1)}, bf16[256,512]{1,0:T(8,128)(2,1)S(1)}, u32[]{:S(2)}, u32[]{:S(2)}) %collective-permute-start.1) | collective-permute-done | bytes 262176 | tf_op jit(solution)/shard_map/ppermute | solution.py:109
  31.0 7.9 %collective-permute-done.2 = bf16[256,512]{1,0:T(8,128)(2,1)S(1)} collective-permute-done((bf16[256,512]{1,0:T(8,128)(2,1)S(1)}, bf16[256,512]{1,0:T(8,128)(2,1)S(1)}, u32[]{:S(2)}, u32[]{:S(2)}) %collective-permute-start.2) | collective-permute-done | bytes 262176 | tf_op jit(solution)/shard_map/ppermute | solution.py:109
  38.9 1.2 reduce-window.14
  40.2 6.3 %collective-permute-done.3 = bf16[256,512]{1,0:T(8,128)(2,1)S(1)} collective-permute-done((bf16[256,512]{1,0:T(8,128)(2,1)S(1)}, bf16[256,512]{1,0:T(8,128)(2,1)S(1)}, u32[]{:S(2)}, u32[]{:S(2)}) %collective-permute-start.3) | collective-permute-done | bytes 262176 | tf_op jit(solution)/shard_map/ppermute | solution.py:109
  46.7 8.3 %collective-permute-done.4 = bf16[256,512]{1,0:T(8,128)(2,1)S(1)} collective-permute-done((bf16[256,512]{1,0:T(8,128)(2,1)S(1)}, bf16[256,512]{1,0:T(8,128)(2,1)S(1)}, u32[]{:S(2)}, u32[]{:S(2)}) %collective-permute-start.4) | collective-permute-done | bytes 262176 | tf_op jit(solution)/shard_map/ppermute | solution.py:109
  55.2 9.4 %collective-permute-done.5 = bf16[256,512]{1,0:T(8,128)(2,1)S(1)} collective-permute-done((bf16[256,512]{1,0:T(8,128)(2,1)S(1)}, bf16[256,512]{1,0:T(8,128)(2,1)S(1)}, u32[]{:S(2)}, u32[]{:S(2)}) %collective-permute-start.5) | collective-permute-done | bytes 262176 | tf_op jit(solution)/shard_map/ppermute | solution.py:109
  64.7 7.5 %collective-permute-done.6 = bf16[256,512]{1,0:T(8,128)(2,1)S(1)} collective-permute-done((bf16[256,512]{1,0:T(8,128)(2,1)S(1)}, bf16[256,512]{1,0:T(8,128)(2,1)S(1)}, u32[]{:S(2)}, u32[]{:S(2)}) %collective-permute-start.6) | collective-permute-done | bytes 262176 | tf_op jit(solution)/shard_map/ppermute | solution.py:109
  84.3 4.1 fusion.1
  88.4 1.1 fusion.21
  91.4 20.9 %all-gather.2 = bf16[32,1,8]{2,1,0:T(2,128)(2,1)S(1)} all-gather(bf16[1,1,8]{2,1,0:T(2,128)(2,1)S(1)} %bitcast.151), channel_id=1, replica_groups=mesh['seq'=32,'tp'=8] {'seq'}, dimensions={0}, use_global_device_ids=true | all-gather | bytes 528 | tf_op jit(solution)/shard_map/all_gather | solution.py:19
  113.5 1.8 fusion.7
  115.3 26.1 %all-gather.15.cloned.1.call-done = bf16[256,128,64]{1,2,0:T(8,128)(2,1)} async-done(((bf16[8,128,64]{1,2,0:T(8,128)(2,1)}), bf16[256,128,64]{1,2,0:T(8,128)(2,1)}) %all-gather.15.cloned.1.call-update) | async-done | bytes 4194320 | tf_op jit(solution)/shard_map/all_gather | solution.py:19
  141.5 32.8 %while.16 = (s32[]{:T(128)}, f32[8,128,64]{2,1,0:T(8,128)S(1)}, s32[]{:T(128)}, bf16[32,8,128,64]{2,3,1,0:T(8,128)(2,1)}, bf16[32,8]{1,0:T(8,128)(2,1)S(1)}, /*index=5*/s32[]{:T(128)}, s32[]{:T(128)}, s32[]{:T(128)}, s32[]{:T(128)}) while((s32[]{:T(128)}, f32[8,128,64]{2,1,0:T(8,128)S(1)}, s32[]{:T(128)}, bf16[32,8,128,64]{2,3,1,0:T(8,128)(2,1)}, ...), condition=%wide.region_5.6_spmd, body=%wide.region_4.5_spmd.sunk | while | flops 196622 | bytes 1179883 | solution.py:34
  142.8 0.9 constant_dynamic-slice_fusion.4
  144.1 0.9 constant_dynamic-slice_fusion.4
  145.4 0.9 constant_dynamic-slice_fusion.4
  146.7 0.9 constant_dynamic-slice_fusion.4
  149.3 0.9 constant_dynamic-slice_fusion.4
  151.9 0.9 constant_dynamic-slice_fusion.4
  153.2 0.9 constant_dynamic-slice_fusion.4
  154.5 0.9 constant_dynamic-slice_fusion.4
  155.8 0.9 constant_dynamic-slice_fusion.4
  158.4 0.9 constant_dynamic-slice_fusion.4
  161.0 0.9 constant_dynamic-slice_fusion.4
  162.3 0.9 constant_dynamic-slice_fusion.4
  163.6 0.9 constant_dynamic-slice_fusion.4
  164.9 0.9 constant_dynamic-slice_fusion.4
  175.3 8.8 %all-gather.13.cloned.1.call-done = bf16[256,4096]{1,0:T(8,128)(2,1)} async-done(((bf16[256,512]{1,0:T(8,128)(2,1)}), bf16[256,4096]{1,0:T(8,128)(2,1)}) %all-gather.13.cloned.1.call-update) | async-done | bytes 2097168 | tf_op jit(solution)/shard_map/all_gather | solution.py:103
  184.2 4.8 fusion
  189.0 6.5 %copy.85 = bf16[4096,512]{1,0:T(8,128)(2,1)} copy(bf16[4096,512]{0,1:T(8,128)(2,1)} %fusion) | data formatting | bytes 8388608
  196.5 87.0 %reduce-scatter.10.cloned.1.call-done = bf16[128,512]{1,0:T(8,128)(2,1)} async-done(((bf16[4096,512]{1,0:T(8,128)(2,1)}), bf16[128,512]{1,0:T(8,128)(2,1)}) %reduce-scatter.10.cloned.1.call-update) | async-done | bytes 131088
  283.4 1.0 copy.86
  285.4 54.8 %all-gather.11.cloned.1.call-done = bf16[4096,512]{0,1:T(8,128)(2,1)} async-done(((bf16[128,512]{0,1:T(8,128)(2,1)}), bf16[4096,512]{0,1:T(8,128)(2,1)}) %all-gather.11.cloned.1.call-update) | async-done | bytes 4194320 | tf_op jit(solution)/shard_map/all_gather | solution.py:101
  340.2 3.5 convolution_multiply_fusion
  344.5 1.1 fusion.20
  345.6 3.5 fusion.8
  349.1 47.4 %all-gather.17.cloned.1.call-done = bf16[256,128,64]{1,2,0:T(8,128)(2,1)} async-done(((bf16[8,128,64]{1,2,0:T(8,128)(2,1)}), bf16[256,128,64]{1,2,0:T(8,128)(2,1)}) %all-gather.17.cloned.1.call-update) | async-done | bytes 4194320 | tf_op jit(solution)/shard_map/all_gather | solution.py:19
  396.6 7.8 %while.17 = (s32[]{:T(128)}, f32[8,128,64]{2,1,0:T(8,128)S(1)}, s32[]{:T(128)}, bf16[32,8]{1,0:T(8,128)(2,1)S(1)}, bf16[32,8,128,64]{2,3,1,0:T(8,128)(2,1)}, /*index=5*/s32[]{:T(128)}, s32[]{:T(128)}, s32[]{:T(128)}) while((s32[]{:T(128)}, f32[8,128,64]{2,1,0:T(8,128)S(1)}, s32[]{:T(128)}, bf16[32,8]{1,0:T(8,128)(2,1)S(1)}, ...), condition=%wide.region_11.12_spmd, body=%wide.region_10.11_spmd.sunk | while | flops 196621 | bytes 1179863 | solution.py:34
  405.4 4.9 convolution_convert_fusion
  410.5 4.9 convolution_convert_fusion.2
  416.3 83.4 %psum.14 = f32[512]{0:T(512)S(1)} all-reduce(f32[512]{0:T(512)S(1)} %get-tuple-element.273), channel_id=1, replica_groups=mesh['seq'=32,'tp'=8] {'seq'}, use_global_device_ids=true, to_apply=%region_9.10 | all-reduce | flops 512 | bytes 4096 | tf_op jit(solution)/shard_map/psum | solution.py:177
  500.2 30.9 %reduce-scatter.12.cloned.1.call-done = bf16[128,512]{1,0:T(8,128)(2,1)} async-done(((bf16[4096,512]{1,0:T(8,128)(2,1)}), bf16[128,512]{1,0:T(8,128)(2,1)}) %reduce-scatter.12.cloned.1.call-update) | async-done | bytes 131088
  531.2 1.0 copy.88
  533.2 17.5 %psum.15 = f32[128]{0:T(128)S(1)} all-reduce(f32[128]{0:T(128)S(1)} %get-tuple-element.275), channel_id=1, replica_groups=mesh['seq'=32,'tp'=8] {'tp'}, use_global_device_ids=true, to_apply=%region_14.15 | all-reduce | flops 128 | bytes 1024 | tf_op jit(solution)/shard_map/psum | solution.py:178
  551.2 25.1 %reduce-scatter.8.cloned.1.call-done = bf16[256,512]{1,0:T(8,128)(2,1)} async-done(((bf16[256,4096]{1,0:T(8,128)(2,1)}), bf16[256,512]{1,0:T(8,128)(2,1)}) %reduce-scatter.8.cloned.1.call-update) | async-done | bytes 262160 | tf_op jit(solution)/shard_map/reduce_scatter | solution.py:172
  (207 shorter events, 51.6 us)
Async XLA Ops:
  7.2 105.4 %copy-start = (bf16[256,128]{1,0:T(8,128)(2,1)S(1)}, bf16[256,128]{1,0:T(8,128)(2,1)}, u32[]{:S(2)}) copy-start(bf16[256,128]{1,0:T(8,128)(2,1)} %param.19) | copy-start | bytes 196612
  7.2 70.3 %copy-start.2 = (bf16[256,512]{1,0:T(8,128)(2,1)S(1)}, bf16[256,512]{1,0:T(8,128)(2,1)}, u32[]{:S(2)}) copy-start(bf16[256,512]{1,0:T(8,128)(2,1)} %param.14) | copy-start | bytes 786436
  7.2 77.1 %all-gather.9.cloned.1.call-start = ((), (), s32[]{:S(2)}) async-start(), calls=%async_computation.3 | async-start | bytes 4325376 | tf_op jit(solution)/shard_map/all_gather | solution.py:102
  9.8 131.6 %all-gather.15.cloned.1.call-start = ((), (), s32[]{:S(2)}) async-start(), calls=%async_computation.7 | async-start | bytes 4325376 | tf_op jit(solution)/shard_map/all_gather | solution.py:19
  9.9 12.5 %collective-permute-start = (bf16[256,512]{1,0:T(8,128)(2,1)}, bf16[256,512]{1,0:T(8,128)(2,1)S(1)}, u32[]{:S(2)}, u32[]{:S(2)}) collective-permute-start(bf16[256,512]{1,0:T(8,128)(2,1)} %param.14), channel_id=1, source_target_pairs={{0,1},{1,2},{2,3},{3,4},{4,5},{5,6},{6,7},{7,0},{8,9},{9,10},{10,1... | collective-permute-start | bytes 786440 | tf_op jit(solution)/shard_map/ppermute | solution.py:109
  22.3 8.7 %collective-permute-start.1 = (bf16[256,512]{1,0:T(8,128)(2,1)S(1)}, bf16[256,512]{1,0:T(8,128)(2,1)S(1)}, u32[]{:S(2)}, u32[]{:S(2)}) collective-permute-start(bf16[256,512]{1,0:T(8,128)(2,1)S(1)} %collective-permute-done), channel_id=1, source_target_pairs={{0,1},{1,2},{2,3},{3,4},{4,5},{5,6},{6,7},{7,0},{8,9},{9,10},{10,1... | collective-permute-start | bytes 786440 | tf_op jit(solution)/shard_map/ppermute | solution.py:109
  31.0 7.9 %collective-permute-start.2 = (bf16[256,512]{1,0:T(8,128)(2,1)S(1)}, bf16[256,512]{1,0:T(8,128)(2,1)S(1)}, u32[]{:S(2)}, u32[]{:S(2)}) collective-permute-start(bf16[256,512]{1,0:T(8,128)(2,1)S(1)} %collective-permute-done.1), channel_id=1, source_target_pairs={{0,1},{1,2},{2,3},{3,4},{4,5},{5,6},{6,7},{7,0},{8,9},{9,10},{10,1... | collective-permute-start | bytes 786440 | tf_op jit(solution)/shard_map/ppermute | solution.py:109
  38.9 7.6 %collective-permute-start.3 = (bf16[256,512]{1,0:T(8,128)(2,1)S(1)}, bf16[256,512]{1,0:T(8,128)(2,1)S(1)}, u32[]{:S(2)}, u32[]{:S(2)}) collective-permute-start(bf16[256,512]{1,0:T(8,128)(2,1)S(1)} %collective-permute-done.2), channel_id=1, source_target_pairs={{0,1},{1,2},{2,3},{3,4},{4,5},{5,6},{6,7},{7,0},{8,9},{9,10},{10,1... | collective-permute-start | bytes 786440 | tf_op jit(solution)/shard_map/ppermute | solution.py:109
  46.5 8.5 %collective-permute-start.4 = (bf16[256,512]{1,0:T(8,128)(2,1)S(1)}, bf16[256,512]{1,0:T(8,128)(2,1)S(1)}, u32[]{:S(2)}, u32[]{:S(2)}) collective-permute-start(bf16[256,512]{1,0:T(8,128)(2,1)S(1)} %collective-permute-done.3), channel_id=1, source_target_pairs={{0,1},{1,2},{2,3},{3,4},{4,5},{5,6},{6,7},{7,0},{8,9},{9,10},{10,1... | collective-permute-start | bytes 786440 | tf_op jit(solution)/shard_map/ppermute | solution.py:109
  55.0 9.6 %collective-permute-start.5 = (bf16[256,512]{1,0:T(8,128)(2,1)S(1)}, bf16[256,512]{1,0:T(8,128)(2,1)S(1)}, u32[]{:S(2)}, u32[]{:S(2)}) collective-permute-start(bf16[256,512]{1,0:T(8,128)(2,1)S(1)} %collective-permute-done.4), channel_id=1, source_target_pairs={{0,1},{1,2},{2,3},{3,4},{4,5},{5,6},{6,7},{7,0},{8,9},{9,10},{10,1... | collective-permute-start | bytes 786440 | tf_op jit(solution)/shard_map/ppermute | solution.py:109
  64.6 7.6 %collective-permute-start.6 = (bf16[256,512]{1,0:T(8,128)(2,1)S(1)}, bf16[256,512]{1,0:T(8,128)(2,1)S(1)}, u32[]{:S(2)}, u32[]{:S(2)}) collective-permute-start(bf16[256,512]{1,0:T(8,128)(2,1)S(1)} %collective-permute-done.5), channel_id=1, source_target_pairs={{0,1},{1,2},{2,3},{3,4},{4,5},{5,6},{6,7},{7,0},{8,9},{9,10},{10,1... | collective-permute-start | bytes 786440 | tf_op jit(solution)/shard_map/ppermute | solution.py:109
  64.7 19.6 %copy-start.10 = (f32[4096]{0:T(1024)S(1)}, f32[4096]{0:T(1024)}, u32[]{:S(2)}) copy-start(f32[4096]{0:T(1024)} %param.18) | copy-start | bytes 49156
  84.3 4.2 copy-start.3
  84.3 6.0 %copy-start.8 = (f32[256,8]{0,1:T(8,128)S(1)}, f32[256,8]{0,1:T(8,128)}, u32[]{:S(2)}) copy-start(f32[256,8]{0,1:T(8,128)} %param.21) | copy-start | bytes 24580
  89.5 94.7 %all-gather.13.cloned.1.call-start = ((), (), s32[]{:S(2)}) async-start(), calls=%async_computation.6 | async-start | bytes 2359296 | tf_op jit(solution)/shard_map/all_gather | solution.py:103
  90.3 193.2 %reduce-scatter.10.cloned.1.call-start = ((), (), s32[]{:S(2)}) async-start(), calls=%async_computation.9 | async-start | bytes 4325376
  112.8 0.7 copy-start.5
  195.5 0.9 copy-start.7
  195.5 89.0 %copy-start.9 = (f32[512]{0:T(512)S(1)}, f32[512]{0:T(512)}, u32[]{:S(2)}) copy-start(f32[512]{0:T(512)} %param.16) | copy-start | bytes 6148
  195.5 144.7 %copy-start.1 = (bf16[256,4096]{1,0:T(8,128)(2,1)S(1)}, bf16[256,4096]{1,0:T(8,128)(2,1)}, u32[]{:S(2)}) copy-start(bf16[256,4096]{1,0:T(8,128)(2,1)} %all-gather.13.cloned.1.call-done) | copy-start | bytes 6291460
  195.5 144.7 %all-gather.11.cloned.1.call-start = ((), (), s32[]{:S(2)}) async-start(), calls=%async_computation.4 | async-start | bytes 4325376 | tf_op jit(solution)/shard_map/all_gather | solution.py:101
  285.4 60.3 %copy-start.6 = (f32[256,256]{1,0:T(8,128)S(1)}, f32[256,256]{1,0:T(8,128)}, u32[]{:S(2)}) copy-start(f32[256,256]{1,0:T(8,128)} %copy-done.5) | copy-start | bytes 786436
  285.4 111.2 %all-gather.17.cloned.1.call-start = ((), (), s32[]{:S(2)}) async-start(), calls=%async_computation.8 | async-start | bytes 4325376 | tf_op jit(solution)/shard_map/all_gather | solution.py:19
  343.7 0.8 copy-start.4
  345.6 185.6 %reduce-scatter.12.cloned.1.call-start = ((), (), s32[]{:S(2)}) async-start(), calls=%async_computation.10 | async-start | bytes 4325376
  410.3 166.0 %reduce-scatter.8.cloned.1.call-start = ((), (), s32[]{:S(2)}) async-start(), calls=%async_computation.5 | async-start | bytes 2359296 | tf_op jit(solution)/shard_map/reduce_scatter | solution.py:172
Sparse Core Ops, SparseCore 0:
  11.1 56.6 all-gather.8
  89.6 51.7 all-gather.14
  143.2 40.8 all-gather.12
  195.6 87.7 reduce-scatter.9
  286.6 53.5 all-gather.10
  345.7 50.7 all-gather.16
  410.5 120.6 reduce-scatter.11
  534.3 41.9 reduce-scatter.7
